TPU v7x, 128 devices: a whole 4x4x4 slice. The times are simulated.
128 devices in a mesh: row: 16 (over y, x_hi, core), col: 8 (over z, x_lo).
Axes of the slice: x: 4 (x_hi: 2, x_lo: 2; x = x_hi * 2 + x_lo), y: 4, z: 4, core: 2. Of those that a mesh axis runs over, the one named last changes fastest.
Arguments:
- layer_input: bfloat16 [8192, 8192], P('row', 'col'), may hold values from -48 to 48
- w_query: bfloat16 [8192, 8192], P('row', 'col'), may hold values from -0.0625 to 0.0625
- w_key: bfloat16 [8192, 1024], P('row', 'col'), may hold values from -0.0625 to 0.0625
- w_value: bfloat16 [8192, 1024], P('row', 'col'), may hold values from -0.0625 to 0.0625
- counts: int32 [64], replicated, may hold values from 1 to 128
- pattern: int32 [64, 4], P('row'), may hold values from 0 to 63, as said below
- cotangent: bfloat16 [8192, 8192], P('row', 'col'), may hold values from -6 to 6
Outputs:
- attended: bfloat16 [8192, 8192], P('row', 'col')
- input_grad: bfloat16 [8192, 8192], P('row', 'col')
Inputs may be any that keep to these rules, and one draw needn't show every extreme that they name: `pattern`: row b lists 4 different blocks, b itself first; every entry lies at a cyclic distance of at most 4 blocks from b, and the second entry exactly at that distance.
All inputs are finite; a program needn't handle non-finite values.
Results may differ from a plain program's by a relative error of at most 0.035.
The roundings to bfloat16 on the way count: a program that leaves them out, or rounds other values in their place, can miss the bound.
Values may be sent and summed in bfloat16 or wider, within the bound.
A program may use at most 128 MiB of HBM per device.

v0:
```python
import jax
import jax.numpy as jnp
from jax import lax
from jax.sharding import PartitionSpec as P

HEADS = 64
KV_HEADS = 8
HEAD_DIM = 128
BLOCK = 128


def padded(block, sides, width):
    for axis, dim in sides:
        count = lax.axis_size(axis)
        forward = [(i, i + 1) for i in range(count - 1)]
        forward.append((count - 1, 0))
        backward = [(target, source) for source, target in forward]
        low = lax.ppermute(
            lax.slice_in_dim(block, block.shape[dim] - width, None, axis=dim), axis, forward
        )
        high = lax.ppermute(lax.slice_in_dim(block, 0, width, axis=dim), axis, backward)
        block = jnp.concatenate([low, block, high], axis=dim)
    return block


def shifted(block, axis, distance):
    devices = range(lax.axis_size(axis))
    route = [((i - distance) % len(devices), i) for i in devices]
    return lax.ppermute(block, axis, route)


def body(layer_input, w_query, w_key, w_value, counts, pattern, cotangent):
    score_scale = HEAD_DIM ** (-0.5)
    group_size = HEADS // KV_HEADS
    tok_rows = layer_input.shape[0]
    per_dev = tok_rows // BLOCK
    block_count = per_dev * lax.axis_size("row")
    myself = lax.axis_index("row")
    all_features = lax.all_gather(layer_input, "col", axis=1, tiled=True)
    full_query = lax.all_gather(w_query, "row", axis=0, tiled=True)
    full_key = lax.all_gather(w_key, "row", axis=0, tiled=True)
    full_value = lax.all_gather(w_value, "row", axis=0, tiled=True)
    query = jnp.dot(all_features, full_query, preferred_element_type=jnp.float32).astype(
        jnp.bfloat16
    )
    keys = jnp.dot(all_features, full_key, preferred_element_type=jnp.float32).astype(jnp.bfloat16)
    values = jnp.dot(all_features, full_value, preferred_element_type=jnp.float32).astype(
        jnp.bfloat16
    )
    kv_heads = keys.shape[1] // HEAD_DIM
    kv_cols = kv_heads * HEAD_DIM
    joined = jnp.concatenate([keys, values], axis=1)
    source = padded(joined, (("row", 0),), tok_rows)
    first_block = myself * per_dev - per_dev
    span_blocks = 3 * per_dev
    nearby = pattern.shape[1]
    local_index = jnp.mod(pattern - first_block, block_count)
    stacked = source.reshape(span_blocks, BLOCK, 2 * kv_cols)
    picked = jnp.take(stacked, local_index, axis=0).reshape(
        per_dev, nearby * BLOCK, 2, kv_heads, HEAD_DIM
    )
    key_blocks = picked[:, :, 0]
    value_blocks = picked[:, :, 1]
    positions = jnp.arange(BLOCK, dtype=jnp.int32)
    key_counts = jnp.take(counts, pattern, axis=0)
    key_live = (positions[None, None, :] < key_counts[:, :, None]).reshape(per_dev, nearby * BLOCK)
    own_counts = lax.dynamic_slice_in_dim(counts, myself * per_dev, per_dev)
    query_live = (positions[None, :] < own_counts[:, None])[:, :, None, None, None]
    query_blocks = query.reshape(per_dev, BLOCK, kv_heads, group_size, HEAD_DIM)
    scores = (
        jnp.einsum(
            "bqkgd,bjkd->bkgqj", query_blocks, key_blocks, preferred_element_type=jnp.float32
        )
        * score_scale
    )
    scores = jnp.where(key_live[:, None, None, None, :], scores, -1e30)
    score_max = jnp.max(scores, axis=-1, keepdims=True)
    exponent = jnp.exp(scores - score_max)
    prob_full = exponent / jnp.sum(exponent, axis=-1, keepdims=True)
    probs_low = prob_full.astype(jnp.bfloat16)
    mixed_out = jnp.einsum(
        "bkgqj,bjkd->bqkgd", probs_low, value_blocks, preferred_element_type=jnp.float32
    )
    attended = (mixed_out * query_live.astype(jnp.float32)).astype(jnp.bfloat16)
    grad_out = cotangent.reshape(
        per_dev, BLOCK, kv_heads, group_size, HEAD_DIM
    ) * query_live.astype(jnp.bfloat16)
    row_delta = jnp.einsum(
        "bqkgd,bqkgd->bkgq", grad_out, attended, preferred_element_type=jnp.float32
    )
    grad_probs = jnp.einsum(
        "bqkgd,bjkd->bkgqj", grad_out, value_blocks, preferred_element_type=jnp.float32
    )
    grad_scores = (prob_full * (grad_probs - row_delta[..., None]) * score_scale).astype(
        jnp.bfloat16
    )
    grad_query = jnp.einsum(
        "bkgqj,bjkd->bqkgd", grad_scores, key_blocks, preferred_element_type=jnp.float32
    )
    grad_query = grad_query.astype(jnp.bfloat16).reshape(tok_rows, -1)
    key_part = jnp.einsum(
        "bkgqj,bqkgd->bjkd", grad_scores, query_blocks, preferred_element_type=jnp.float32
    )
    value_part = jnp.einsum(
        "bkgqj,bqkgd->bjkd", probs_low, grad_out, preferred_element_type=jnp.float32
    )
    grad_parts = jnp.concatenate(
        [
            key_part.reshape(per_dev * nearby, BLOCK, kv_cols),
            value_part.reshape(per_dev * nearby, BLOCK, kv_cols),
        ],
        axis=-1,
    )
    owed_grads = (
        jnp.zeros((span_blocks, BLOCK, 2 * kv_cols), jnp.float32)
        .at[local_index.reshape(-1)]
        .add(grad_parts)
    )
    from_next = shifted(owed_grads[:per_dev].astype(jnp.bfloat16), "row", -1).astype(jnp.float32)
    from_prev = shifted(owed_grads[2 * per_dev :].astype(jnp.bfloat16), "row", 1).astype(
        jnp.float32
    )
    settled = owed_grads[per_dev : 2 * per_dev] + from_next + from_prev
    settled = settled.reshape(tok_rows, 2 * kv_cols)
    grad_keys = settled[:, :kv_cols].astype(jnp.bfloat16)
    grad_values = settled[:, kv_cols:].astype(jnp.bfloat16)
    contract = (((1,), (1,)), ((), ()))
    partial_grad = lax.dot_general(
        grad_query, full_query, contract, preferred_element_type=jnp.float32
    )
    partial_grad = partial_grad + lax.dot_general(
        grad_keys, full_key, contract, preferred_element_type=jnp.float32
    )
    partial_grad = partial_grad + lax.dot_general(
        grad_values, full_value, contract, preferred_element_type=jnp.float32
    )
    input_grad = lax.psum_scatter(
        partial_grad.astype(jnp.bfloat16), "col", scatter_dimension=1, tiled=True
    )
    return (attended.reshape(tok_rows, -1), input_grad)


def solution(mesh):
    placed = (
        P("row", "col"),
        P("row", "col"),
        P("row", "col"),
        P("row", "col"),
        P(),
        P("row", None),
        P("row", "col"),
    )
    return jax.shard_map(
        body,
        mesh=mesh,
        in_specs=placed,
        out_specs=(P("row", "col"), P("row", "col")),
        check_vma=False,
    )
```

profile of v0, /device:TPU:1, one launch (start us, length us, event | category | flops | bytes accessed | tf_op | source)
XLA Modules:
  0.0 668.0 jit_solution(15478223276111546973)
XLA Ops:
  7.2 0.7 all-gather.9.cloned.1.call-update
  7.9 0.7 all-gather.5.cloned.1.call-update
  8.6 0.0 all-gather.7.cloned.1.call-start
  8.7 0.7 all-gather.7.cloned.1.call-update
  9.4 0.5 all-gather.11.cloned.1.call-update
  10.0 0.0 reduce-scatter.2.cloned.1.call-start
  10.0 0.7 compare_select_fusion
  10.7 0.1 reshape.230
  10.8 0.7 compare_and_fusion
  11.5 0.1 reshape.215
  11.6 0.1 reshape.222
  11.7 0.7 dynamic_slice.3
  12.4 1.3 gather_fusion.1
  13.7 0.1 reshape.229
  13.8 0.1 broadcast_bitcast_fusion.1
  13.9 0.1 fusion.36
  14.0 0.7 and_select_fusion
  14.6 0.1 broadcast_bitcast_fusion
  14.7 46.9 %all-gather.9.cloned.1.call-done = bf16[8192,128]{1,0:T(8,128)(2,1)} async-done(((bf16[512,128]{1,0:T(8,128)(2,1)}), bf16[8192,128]{1,0:T(8,128)(2,1)}) %all-gather.9.cloned.1.call-update) | async-done | bytes 2097168 | tf_op jit(solution)/shard_map/all_gather | solution.py:42
  61.6 168.4 %all-gather.5.cloned.1.call-done = bf16[512,8192]{1,0:T(8,128)(2,1)} async-done(((bf16[512,1024]{1,0:T(8,128)(2,1)}), bf16[512,8192]{1,0:T(8,128)(2,1)}) %all-gather.5.cloned.1.call-update) | async-done | bytes 8388624 | tf_op jit(solution)/shard_map/all_gather | solution.py:39
  230.0 6.9 %convolution_convert_fusion.2 = bf16[512,128]{0,1:T(8,128)(2,1)S(1)} fusion(bf16[512,8192]{1,0:T(8,128)(2,1)} %all-gather.5.cloned.1.call-done, bf16[8192,128]{1,0:T(8,128)(2,1)} %all-gather.9.cloned.1.call-done), kind=kOutput, calls=%fused_computation.31 | convolution fusion | flops 1073807360 | bytes 10616832 | tf_op jit(solution)/shard_map/dot_general | solution.py:47
  236.8 44.6 %all-gather.7.cloned.1.call-done = bf16[8192,128]{1,0:T(8,128)(2,1)} async-done(((bf16[512,128]{1,0:T(8,128)(2,1)}), bf16[8192,128]{1,0:T(8,128)(2,1)}) %all-gather.7.cloned.1.call-update) | async-done | bytes 2097168 | tf_op jit(solution)/shard_map/all_gather | solution.py:41
  281.4 6.9 %convolution_convert_fusion.3 = bf16[512,128]{0,1:T(8,128)(2,1)S(1)} fusion(bf16[512,8192]{1,0:T(8,128)(2,1)} %all-gather.5.cloned.1.call-done, bf16[8192,128]{1,0:T(8,128)(2,1)} %all-gather.7.cloned.1.call-done), kind=kOutput, calls=%fused_computation.32 | convolution fusion | flops 1073807360 | bytes 10616832 | tf_op jit(solution)/shard_map/dot_general | solution.py:46
  288.3 0.3 collective-permute-start.1
  288.6 3.0 collective-permute-start
  291.6 0.3 copy.63
  291.9 1.6 copy.25
  293.5 5.3 collective-permute-done.1
  298.8 2.7 collective-permute-done
  301.5 0.1 pad_maximum_fusion.1
  301.6 0.3 copy.19
  301.8 0.6 gather_fusion
  302.4 0.3 gather.11
  302.7 0.5 copy_select_fusion
  303.2 91.0 %all-gather.11.cloned.1.call-done = bf16[8192,1024]{1,0:T(8,128)(2,1)} async-done(((bf16[512,1024]{1,0:T(8,128)(2,1)}), bf16[8192,1024]{1,0:T(8,128)(2,1)}) %all-gather.11.cloned.1.call-update) | async-done | bytes 16777232 | tf_op jit(solution)/shard_map/all_gather | solution.py:40
  394.3 14.8 %fusion.16 = bf16[64,8,8,128]{3,1,2,0:T(8,128)(2,1)S(1)} fusion(bf16[512,8192]{1,0:T(8,128)(2,1)} %all-gather.5.cloned.1.call-done, bf16[8192,1024]{1,0:T(8,128)(2,1)} %all-gather.11.cloned.1.call-done), kind=kOutput, calls=%fused_computation.27 | convolution fusion | flops 8590458880 | bytes 26214400 | tf_op jit(solution)/shard_map/dot_general | solution.py:43
  409.0 0.3 copy.61
  409.3 1.9 bitcast_reduce_fusion
  411.2 1.9 fusion.5
  413.2 4.3 fusion.18
  417.5 4.0 fusion.12
  421.4 3.7 fusion.6
  425.2 2.0 copy-done
  427.1 1.8 fusion.17
  428.9 8.0 %copy.49 = bf16[4,8,128,512]{3,1,2,0:T(8,128)(2,1)} copy(bf16[4,8,128,512]{2,3,1,0:T(8,128)(2,1)} %copy-done) | data formatting | bytes 8388608 | tf_op jit(solution)/shard_map/reshape.34
  436.9 0.3 copy.34
  437.2 3.1 convolution_bitcast_fusion
  440.3 0.3 copy.32
  440.6 2.4 copy.29
  443.0 1.5 pad_maximum_fusion
  444.5 0.1 broadcast_in_dim.52
  444.7 3.5 scatter_fusion
  448.2 0.1 convert.8
  448.3 0.7 fusion.42
  449.0 0.2 collective-permute-start.2
  449.3 3.0 collective-permute-start.3
  452.3 15.7 %fusion.21 = f32[512,8192]{1,0:T(8,128)} fusion(bf16[8192,1024]{1,0:T(8,128)(2,1)} %all-gather.11.cloned.1.call-done, bf16[64,8,8,128]{3,2,1,0:T(8,128)(2,1)S(1)} %bitcast.184), kind=kOutput, calls=%fused_computation.33 | convolution fusion | flops 8589934592 | bytes 34603008 | tf_op jit(solution)/shard_map/dot_general | solution.py:128
  468.0 0.1 fusion.29
  468.1 9.8 %fusion.33 = f32[512,8192]{1,0:T(8,128)} fusion(bf16[8192,128]{1,0:T(8,128)(2,1)} %all-gather.7.cloned.1.call-done, bf16[512,256]{1,0:T(8,128)(2,1)S(1)} %bitcast.180), kind=kOutput, calls=%fused_computation.52 | convolution fusion | flops 1073741824 | bytes 19005440 | tf_op jit(solution)/shard_map/dot_general | solution.py:131
  477.9 15.3 %add_convert_fusion = bf16[512,8192]{1,0:T(8,128)(2,1)} fusion(f32[512,8192]{1,0:T(8,128)} %fusion.21, f32[512,8192]{1,0:T(8,128)} %fusion.33, bf16[8192,128]{1,0:T(8,128)(2,1)S(1)} %copy-done.1, bf16[512,256]{1,0:T(8,128)(2,1)S(1)} %bitcast.181), kind=kOutput, calls=%fused_computation.3 | convolution fusion | flops 1086324736 | bytes 44171264 | tf_op jit(solution)/shard_map/dot_general | solution.py:134
  493.2 1.2 copy-done.3
  494.4 0.7 copy.24
  495.1 1.2 copy.77
  496.4 165.0 %reduce-scatter.2.cloned.1.call-done = bf16[512,1024]{1,0:T(8,128)(2,1)} async-done(((bf16[512,8192]{1,0:T(8,128)(2,1)}), bf16[512,1024]{1,0:T(8,128)(2,1)}) %reduce-scatter.2.cloned.1.call-update) | async-done | bytes 1048592 | tf_op jit(solution)/shard_map/reduce_scatter | solution.py:137
  (26 shorter events, 0.2 us)
Async XLA Ops:
  7.2 54.4 %all-gather.9.cloned.1.call-start = ((), (), s32[]{:S(2)}) async-start(), calls=%async_computation.3 | async-start | bytes 2228224 | tf_op jit(solution)/shard_map/all_gather | solution.py:42
  7.9 222.1 %all-gather.5.cloned.1.call-start = ((), (), s32[]{:S(2)}) async-start(), calls=%async_computation.1 | async-start | bytes 9437184 | tf_op jit(solution)/shard_map/all_gather | solution.py:39
  8.6 272.8 %all-gather.7.cloned.1.call-start = ((), (), s32[]{:S(2)}) async-start(), calls=%async_computation.2 | async-start | bytes 2228224 | tf_op jit(solution)/shard_map/all_gather | solution.py:41
  9.4 384.9 %all-gather.11.cloned.1.call-start = ((), (), s32[]{:S(2)}) async-start(), calls=%async_computation.4 | async-start | bytes 17825792 | tf_op jit(solution)/shard_map/all_gather | solution.py:40
  10.0 651.5 %reduce-scatter.2.cloned.1.call-start = ((), (), s32[]{:S(2)}) async-start(), calls=%async_computation.5 | async-start | bytes 9437184 | tf_op jit(solution)/shard_map/reduce_scatter | solution.py:137
  14.7 276.9 %copy-start.2 = (bf16[512,1024]{1,0:T(8,128)(2,1)S(1)}, bf16[512,1024]{1,0:T(8,128)(2,1)}, u32[]{:S(2)}) copy-start(bf16[512,1024]{1,0:T(8,128)(2,1)} %param.13) | copy-start | bytes 3145732
  288.3 10.5 %collective-permute-start.1 = (bf16[512,256]{0,1:T(8,128)(2,1)S(1)}, bf16[512,256]{0,1:T(8,128)(2,1)S(1)}, u32[]{:S(2)}, u32[]{:S(2)}) collective-permute-start(bf16[512,256]{0,1:T(8,128)(2,1)S(1)} %pad_maximum_fusion.2), channel_id=1, source_target_pairs={{8,0},{16,8},{24,16},{32,24},{40,32},{48,40},{56,48},{64,56},{72,6... | collective-permute-start | bytes 786440 | tf_op jit(solution)/shard_map/ppermute | solution.py:21
  288.6 12.9 %collective-permute-start = (bf16[512,256]{0,1:T(8,128)(2,1)S(1)}, bf16[512,256]{0,1:T(8,128)(2,1)S(1)}, u32[]{:S(2)}, u32[]{:S(2)}) collective-permute-start(bf16[512,256]{0,1:T(8,128)(2,1)S(1)} %pad_maximum_fusion.2), channel_id=1, source_target_pairs={{0,8},{8,16},{16,24},{24,32},{32,40},{40,48},{48,56},{56,64},{64,7... | collective-permute-start | bytes 786440 | tf_op jit(solution)/shard_map/ppermute | solution.py:18
  409.3 3.8 copy-start.4
  425.2 2.0 copy-start
  428.9 8.0 %copy-start.6 = (f32[4,512,1,128]{1,3,0,2:T(8,128)S(1)}, f32[4,512,1,128]{1,3,0,2:T(8,128)}, u32[]{:S(2)}) copy-start(f32[4,512,1,128]{1,3,0,2:T(8,128)} %fusion.18) | copy-start | bytes 3145732
  444.5 7.8 %copy-start.5 = (bf16[4,128,1,8,128]{4,3,1,0,2:T(8,128)(2,1)S(1)}, bf16[4,128,1,8,128]{4,3,1,0,2:T(8,128)(2,1)}, u32[]{:S(2)}) copy-start(bf16[4,128,1,8,128]{4,3,1,0,2:T(8,128)(2,1)} %copy.29) | copy-start | bytes 3145732
  449.0 19.0 %collective-permute-start.2 = (bf16[4,128,256]{2,1,0:T(8,128)(2,1)}, bf16[4,128,256]{2,1,0:T(8,128)(2,1)S(1)}, u32[]{:S(2)}, u32[]{:S(2)}) collective-permute-start(bf16[4,128,256]{2,1,0:T(8,128)(2,1)} %get-tuple-element.4), channel_id=1, source_target_pairs={{8,0},{16,8},{24,16},{32,24},{40,32},{48,40},{56,48},{64,56},{72,6... | collective-permute-start | bytes 786440 | tf_op jit(solution)/shard_map/ppermute | solution.py:29
  449.3 18.7 %collective-permute-start.3 = (bf16[4,128,256]{2,1,0:T(8,128)(2,1)S(1)}, bf16[4,128,256]{2,1,0:T(8,128)(2,1)S(1)}, u32[]{:S(2)}, u32[]{:S(2)}) collective-permute-start(bf16[4,128,256]{2,1,0:T(8,128)(2,1)S(1)} %get-tuple-element.5), channel_id=1, source_target_pairs={{120,0},{0,8},{8,16},{16,24},{24,32},{32,40},{40,48},{48,56},{56,6... | collective-permute-start | bytes 786440 | tf_op jit(solution)/shard_map/ppermute | solution.py:29
  468.1 9.8 %copy-start.1 = (bf16[8192,128]{1,0:T(8,128)(2,1)S(1)}, bf16[8192,128]{1,0:T(8,128)(2,1)}, u32[]{:S(2)}) copy-start(bf16[8192,128]{1,0:T(8,128)(2,1)} %all-gather.9.cloned.1.call-done) | copy-start | bytes 6291460
  493.2 1.2 copy-start.3
Sparse Core Ops, SparseCore 0:
  10.5 51.0 all-gather.8
  63.2 166.7 all-gather.4
  232.4 48.9 all-gather.6
  283.7 110.4 all-gather.10
  493.4 168.0 reduce-scatter.1
where the time goes:
time: 668 us
  waiting for transfers between devices  526 us (79%)
  matrix products  88 us (13%)
  local copies, waits for them, and re-layouts  22.9 us (3%)
  between operations  14 us (2%)
  other arithmetic  9.83 us (1%)
  starting transfers between devices  6.76 us (1%)
    all_gather x1, waiting for transfers between devices, body(): all_features = lax.all_gather(layer_input, 'col', axis=1, tiled=True)  168 us
    reduce_scatter x1, waiting for transfers between devices, body(): lax.psum_scatter(partial_grad.astype(jnp.bfloat16), 'col', scatter_dimens...  165 us
    all_gather x1, waiting for transfers between devices, body(): full_query = lax.all_gather(w_query, 'row', axis=0, tiled=True)  91 us
    all_gather x1, waiting for transfers between devices, body(): full_value = lax.all_gather(w_value, 'row', axis=0, tiled=True)  46.9 us
    all_gather x1, waiting for transfers between devices, body(): full_key = lax.all_gather(w_key, 'row', axis=0, tiled=True)  44.6 us
    dot_general x1, matrix products, body(): lax.dot_general(grad_query, full_query, contract, preferred_element_type=...  15.7 us
    dot_general x1, matrix products, body(): lax.dot_general(grad_values, full_value, contract, preferred_element_type...  15.3 us
    dot_general x1, matrix products, body(): jnp.dot(all_features, full_query, preferred_element_type=jnp.float32)  14.8 us
  transfers between devices with their start and end apart: 9, of which 7 were waited for; matrix products, arithmetic and copies ran while one was open for 6% of the time, Pallas kernels for 0%

commit v1 on v0

--- a/solution.py
+++ b/solution.py
@@ -39,7 +39,9 @@
     all_features = lax.all_gather(layer_input, "col", axis=1, tiled=True)
     full_query = lax.all_gather(w_query, "row", axis=0, tiled=True)
     full_key = lax.all_gather(w_key, "row", axis=0, tiled=True)
-    full_value = lax.all_gather(w_value, "row", axis=0, tiled=True)
+    full_value = jnp.concatenate(
+        lax.all_to_all(jnp.stack([w_value] * lax.axis_size("row")), "row", 0, 0), axis=0
+    )
     query = jnp.dot(all_features, full_query, preferred_element_type=jnp.float32).astype(
         jnp.bfloat16
     )

time: 668 us -> 634 us (0.949)
  waiting for transfers between devices: 526 us -> 479 us
  starting transfers between devices: 6.76 us -> 15.1 us
    all_gather x1 -> x0, waiting for transfers between devices: 46.9 us -> none  [body(): full_value = lax.all_gather(w_value, 'row', axis=0, tiled=True)]
    all_to_all x0 -> x1, starting transfers between devices: none -> 8.45 us  [body(): lax.all_to_all(jnp.stack([w_value] * lax.axis_size('row')), 'row', 0, 0)]
    all_gather x1, waiting for transfers between devices: 91 us -> 84.2 us  [body(): full_query = lax.all_gather(w_query, 'row', axis=0, tiled=True)]
  transfers between devices with their start and end apart: 9 -> 9, of which waited for: 7 -> 5; matrix products, arithmetic and copies ran while one was open for 6% -> 7% of each run, Pallas kernels for 0% -> 0%
where the time goes in v1:
time: 634 us
  waiting for transfers between devices  479 us (76%)
  matrix products  88.1 us (14%)
  local copies, waits for them, and re-layouts  26.7 us (4%)
  starting transfers between devices  15.1 us (2%)
  between operations  14 us (2%)
  other arithmetic  10.4 us (2%)
    all_gather x1, waiting for transfers between devices, body(): all_features = lax.all_gather(layer_input, 'col', axis=1, tiled=True)  168 us
    reduce_scatter x1, waiting for transfers between devices, body(): lax.psum_scatter(partial_grad.astype(jnp.bfloat16), 'col', scatter_dimens...  165 us
    all_gather x1, waiting for transfers between devices, body(): full_query = lax.all_gather(w_query, 'row', axis=0, tiled=True)  84.2 us
    all_gather x1, waiting for transfers between devices, body(): full_key = lax.all_gather(w_key, 'row', axis=0, tiled=True)  51.1 us
    dot_general x1, matrix products, body(): lax.dot_general(grad_query, full_query, contract, preferred_element_type=...  15.7 us
    dot_general x1, matrix products, body(): lax.dot_general(grad_values, full_value, contract, preferred_element_type...  15.3 us
    dot_general x1, matrix products, body(): jnp.dot(all_features, full_query, preferred_element_type=jnp.float32)  14.8 us
  transfers between devices with their start and end apart: 9, of which 5 were waited for; matrix products, arithmetic and copies ran while one was open for 7% of the time, Pallas kernels for 0%

profile of v1, /device:TPU:1, one launch (start us, length us, event | category | flops | bytes accessed | tf_op | source)
XLA Modules:
  0.0 633.8 jit_solution(8201716171322576729)
XLA Ops:
  7.2 0.0 all-gather.6.cloned.1.call-start
  7.2 0.7 all-gather.6.cloned.1.call-update
  7.9 0.0 all-gather.4.cloned.1.call-start
  8.0 0.7 all-gather.4.cloned.1.call-update
  8.7 0.0 all-gather.8.cloned.1.call-start
  8.7 0.7 all-gather.8.cloned.1.call-update
  9.4 2.7 stack.2
  12.1 8.4 %all-to-all-start = ((bf16[16,512,128]{2,1,0:T(8,128)(2,1)}), bf16[16,512,128]{2,1,0:T(8,128)(2,1)S(1)}, u32[]{:S(2)}, u32[]{:S(2)}) async-start(bf16[16,512,128]{2,1,0:T(8,128)(2,1)} %stack.2), calls=%async_computation | async-start | bytes 4194304 | tf_op jit(solution)/shard_map/all_to_all | solution.py:43
  20.5 0.0 reduce-scatter.2.cloned.1.call-start
  20.6 0.1 reshape.236
  20.7 0.1 reshape.221
  20.8 0.1 reshape.228
  20.9 0.1 dynamic_slice.3
  21.0 0.7 gather_fusion.1
  21.6 0.1 reshape.235
  21.7 0.1 broadcast_bitcast_fusion.1
  21.8 0.1 fusion.36
  21.9 0.1 broadcast_bitcast_fusion
  22.0 51.1 %all-gather.6.cloned.1.call-done = bf16[8192,128]{1,0:T(8,128)(2,1)} async-done(((bf16[512,128]{1,0:T(8,128)(2,1)}), bf16[8192,128]{1,0:T(8,128)(2,1)}) %all-gather.6.cloned.1.call-update) | async-done | bytes 2097168 | tf_op jit(solution)/shard_map/all_gather | solution.py:41
  73.0 168.4 %all-gather.4.cloned.1.call-done = bf16[512,8192]{1,0:T(8,128)(2,1)} async-done(((bf16[512,1024]{1,0:T(8,128)(2,1)}), bf16[512,8192]{1,0:T(8,128)(2,1)}) %all-gather.4.cloned.1.call-update) | async-done | bytes 8388624 | tf_op jit(solution)/shard_map/all_gather | solution.py:39
  241.5 6.8 %convolution_convert_fusion.3 = bf16[512,128]{0,1:T(8,128)(2,1)S(1)} fusion(bf16[512,8192]{1,0:T(8,128)(2,1)} %all-gather.4.cloned.1.call-done, bf16[8192,128]{1,0:T(8,128)(2,1)} %all-gather.6.cloned.1.call-done), kind=kOutput, calls=%fused_computation.32 | convolution fusion | flops 1073807360 | bytes 10616832 | tf_op jit(solution)/shard_map/dot_general | solution.py:48
  248.3 7.1 %convolution_convert_fusion.2 = bf16[512,128]{0,1:T(8,128)(2,1)S(1)} fusion(bf16[512,8192]{1,0:T(8,128)(2,1)} %all-gather.4.cloned.1.call-done, bf16[8192,128]{1,0:T(8,128)(2,1)S(1)} %bitcast.174), kind=kOutput, calls=%fused_computation.31 | convolution fusion | flops 1073807360 | bytes 10616832 | tf_op jit(solution)/shard_map/dot_general | solution.py:49
  255.4 0.7 pad_maximum_fusion.2
  256.1 0.7 collective-permute-start.1
  256.8 2.6 collective-permute-start
  259.4 1.5 copy.63
  260.9 1.6 copy.25
  262.5 8.6 %collective-permute-done.1 = bf16[512,256]{0,1:T(8,128)(2,1)} collective-permute-done((bf16[512,256]{0,1:T(8,128)(2,1)}, bf16[512,256]{0,1:T(8,128)(2,1)}, u32[]{:S(2)}, u32[]{:S(2)}) %collective-permute-start.1) | collective-permute-done | bytes 262176 | tf_op jit(solution)/shard_map/ppermute | solution.py:21
  271.2 2.0 pad_maximum_fusion.1
  273.1 1.4 copy.19
  274.6 0.6 gather_fusion
  275.2 0.3 gather.11
  275.5 0.5 copy_select_fusion
  276.0 84.2 %all-gather.8.cloned.1.call-done = bf16[8192,1024]{1,0:T(8,128)(2,1)} async-done(((bf16[512,1024]{1,0:T(8,128)(2,1)}), bf16[8192,1024]{1,0:T(8,128)(2,1)}) %all-gather.8.cloned.1.call-update) | async-done | bytes 16777232 | tf_op jit(solution)/shard_map/all_gather | solution.py:40
  360.2 14.8 %fusion.16 = bf16[64,8,8,128]{3,1,2,0:T(8,128)(2,1)S(1)} fusion(bf16[512,8192]{1,0:T(8,128)(2,1)} %all-gather.4.cloned.1.call-done, bf16[8192,1024]{1,0:T(8,128)(2,1)} %all-gather.8.cloned.1.call-done), kind=kOutput, calls=%fused_computation.27 | convolution fusion | flops 8590458880 | bytes 26214400 | tf_op jit(solution)/shard_map/dot_general | solution.py:45
  375.0 0.3 copy.61
  375.2 1.9 bitcast_reduce_fusion
  377.1 1.9 fusion.5
  379.1 4.3 fusion.18
  383.4 4.0 fusion.12
  387.3 3.7 fusion.6
  391.1 2.0 copy-done.1
  393.0 1.8 fusion.17
  394.8 8.0 %copy.49 = bf16[4,8,128,512]{3,1,2,0:T(8,128)(2,1)} copy(bf16[4,8,128,512]{2,3,1,0:T(8,128)(2,1)} %copy-done.1) | data formatting | bytes 8388608 | tf_op jit(solution)/shard_map/reshape.36
  402.8 0.3 copy.34
  403.1 3.1 convolution_bitcast_fusion
  406.2 0.3 copy.32
  406.5 2.4 copy.29
  408.9 1.5 pad_maximum_fusion
  410.4 0.1 broadcast_in_dim.52
  410.6 3.5 scatter_fusion
  414.1 0.1 convert.8
  414.2 0.7 fusion.42
  414.9 0.2 collective-permute-start.2
  415.2 3.0 collective-permute-start.3
  418.2 15.7 %fusion.21 = f32[512,8192]{1,0:T(8,128)} fusion(bf16[8192,1024]{1,0:T(8,128)(2,1)} %all-gather.8.cloned.1.call-done, bf16[64,8,8,128]{3,2,1,0:T(8,128)(2,1)S(1)} %bitcast.187), kind=kOutput, calls=%fused_computation.33 | convolution fusion | flops 8589934592 | bytes 34603008 | tf_op jit(solution)/shard_map/dot_general | solution.py:130
  433.8 0.1 fusion.29
  433.9 9.8 %fusion.33 = f32[512,8192]{1,0:T(8,128)} fusion(bf16[8192,128]{1,0:T(8,128)(2,1)} %all-gather.6.cloned.1.call-done, bf16[512,256]{1,0:T(8,128)(2,1)S(1)} %bitcast.183), kind=kOutput, calls=%fused_computation.52 | convolution fusion | flops 1073741824 | bytes 19005440 | tf_op jit(solution)/shard_map/dot_general | solution.py:133
  443.8 15.3 %add_convert_fusion = bf16[512,8192]{1,0:T(8,128)(2,1)} fusion(f32[512,8192]{1,0:T(8,128)} %fusion.21, f32[512,8192]{1,0:T(8,128)} %fusion.33, bf16[8192,128]{1,0:T(8,128)(2,1)S(1)} %bitcast.175, bf16[512,256]{1,0:T(8,128)(2,1)S(1)} %bitcast.184), kind=kOutput, calls=%fused_computation.3 | convolution fusion | flops 1086324736 | bytes 44171264 | tf_op jit(solution)/shard_map/dot_general | solution.py:136
  459.1 0.0 reduce-scatter.2.cloned.1.call-update
  459.1 1.2 copy-done.4
  460.3 0.7 copy.24
  461.0 1.2 copy.77
  462.2 165.0 %reduce-scatter.2.cloned.1.call-done = bf16[512,1024]{1,0:T(8,128)(2,1)} async-done(((bf16[512,8192]{1,0:T(8,128)(2,1)}), bf16[512,1024]{1,0:T(8,128)(2,1)}) %reduce-scatter.2.cloned.1.call-update) | async-done | bytes 1048592 | tf_op jit(solution)/shard_map/reduce_scatter | solution.py:139
  (30 shorter events, 0.1 us)
Async XLA Ops:
  7.2 13.4 %copy-start.8 = (s32[4,4]{1,0:T(4,128)S(1)}, s32[4,4]{1,0:T(4,128)}, u32[]{:S(2)}) copy-start(s32[4,4]{1,0:T(4,128)} %param.12) | copy-start | bytes 196
  7.2 13.7 %copy-start = (s32[64]{0:T(128)S(1)}, s32[64]{0:T(128)}, u32[]{:S(2)}) copy-start(s32[64]{0:T(128)} %param.11) | copy-start | bytes 772
  7.2 65.9 %all-gather.6.cloned.1.call-start = ((), (), s32[]{:S(2)}) async-start(), calls=%async_computation.3 | async-start | bytes 2228224 | tf_op jit(solution)/shard_map/all_gather | solution.py:41
  7.9 233.5 %all-gather.4.cloned.1.call-start = ((), (), s32[]{:S(2)}) async-start(), calls=%async_computation.2 | async-start | bytes 9437184 | tf_op jit(solution)/shard_map/all_gather | solution.py:39
  8.7 351.5 %all-gather.8.cloned.1.call-start = ((), (), s32[]{:S(2)}) async-start(), calls=%async_computation.4 | async-start | bytes 17825792 | tf_op jit(solution)/shard_map/all_gather | solution.py:40
  12.1 236.2 %all-to-all-start = ((bf16[16,512,128]{2,1,0:T(8,128)(2,1)}), bf16[16,512,128]{2,1,0:T(8,128)(2,1)S(1)}, u32[]{:S(2)}, u32[]{:S(2)}) async-start(bf16[16,512,128]{2,1,0:T(8,128)(2,1)} %stack.2), calls=%async_computation | async-start | bytes 4194304 | tf_op jit(solution)/shard_map/all_to_all | solution.py:43
  20.5 606.7 %reduce-scatter.2.cloned.1.call-start = ((), (), s32[]{:S(2)}) async-start(), calls=%async_computation.5 | async-start | bytes 9437184 | tf_op jit(solution)/shard_map/reduce_scatter | solution.py:139
  248.3 24.8 %copy-start.2 = (bf16[16,512,128]{2,1,0:T(8,128)(2,1)}, bf16[16,512,128]{2,1,0:T(8,128)(2,1)S(1)}, u32[]{:S(2)}) copy-start(bf16[16,512,128]{2,1,0:T(8,128)(2,1)S(1)} %all-to-all-done) | copy-start | bytes 6291460
  256.1 15.0 %collective-permute-start.1 = (bf16[512,256]{0,1:T(8,128)(2,1)}, bf16[512,256]{0,1:T(8,128)(2,1)}, u32[]{:S(2)}, u32[]{:S(2)}) collective-permute-start(bf16[512,256]{0,1:T(8,128)(2,1)} %pad_maximum_fusion.2), channel_id=1, source_target_pairs={{8,0},{16,8},{24,16},{32,24},{40,32},{48,40},{56,48},{64,56},{72,6... | collective-permute-start | bytes 786440 | tf_op jit(solution)/shard_map/ppermute | solution.py:21
  256.8 14.4 %collective-permute-start = (bf16[512,256]{0,1:T(8,128)(2,1)}, bf16[512,256]{0,1:T(8,128)(2,1)}, u32[]{:S(2)}, u32[]{:S(2)}) collective-permute-start(bf16[512,256]{0,1:T(8,128)(2,1)} %pad_maximum_fusion.2), channel_id=1, source_target_pairs={{0,8},{8,16},{16,24},{24,32},{32,40},{40,48},{48,56},{56,64},{64,7... | collective-permute-start | bytes 786440 | tf_op jit(solution)/shard_map/ppermute | solution.py:18
  375.2 3.8 copy-start.5
  391.0 2.0 copy-start.1
  394.8 8.0 %copy-start.7 = (f32[4,512,1,128]{1,3,0,2:T(8,128)S(1)}, f32[4,512,1,128]{1,3,0,2:T(8,128)}, u32[]{:S(2)}) copy-start(f32[4,512,1,128]{1,3,0,2:T(8,128)} %fusion.18) | copy-start | bytes 3145732
  410.4 7.8 %copy-start.6 = (bf16[4,128,1,8,128]{4,3,1,0,2:T(8,128)(2,1)S(1)}, bf16[4,128,1,8,128]{4,3,1,0,2:T(8,128)(2,1)}, u32[]{:S(2)}) copy-start(bf16[4,128,1,8,128]{4,3,1,0,2:T(8,128)(2,1)} %copy.29) | copy-start | bytes 3145732
  414.9 18.9 %collective-permute-start.2 = (bf16[4,128,256]{2,1,0:T(8,128)(2,1)}, bf16[4,128,256]{2,1,0:T(8,128)(2,1)S(1)}, u32[]{:S(2)}, u32[]{:S(2)}) collective-permute-start(bf16[4,128,256]{2,1,0:T(8,128)(2,1)} %get-tuple-element.4), channel_id=1, source_target_pairs={{8,0},{16,8},{24,16},{32,24},{40,32},{48,40},{56,48},{64,56},{72,6... | collective-permute-start | bytes 786440 | tf_op jit(solution)/shard_map/ppermute | solution.py:29
  415.2 18.7 %collective-permute-start.3 = (bf16[4,128,256]{2,1,0:T(8,128)(2,1)S(1)}, bf16[4,128,256]{2,1,0:T(8,128)(2,1)S(1)}, u32[]{:S(2)}, u32[]{:S(2)}) collective-permute-start(bf16[4,128,256]{2,1,0:T(8,128)(2,1)S(1)} %get-tuple-element.5), channel_id=1, source_target_pairs={{120,0},{0,8},{8,16},{16,24},{24,32},{32,40},{40,48},{48,56},{56,6... | collective-permute-start | bytes 786440 | tf_op jit(solution)/shard_map/ppermute | solution.py:29
  433.9 9.8 %copy-start.3 = (bf16[16,512,128]{2,1,0:T(8,128)(2,1)S(1)}, bf16[16,512,128]{2,1,0:T(8,128)(2,1)}, u32[]{:S(2)}) copy-start(bf16[16,512,128]{2,1,0:T(8,128)(2,1)} %copy-done.2) | copy-start | bytes 6291460
  459.1 1.2 copy-start.4
Sparse Core Ops, SparseCore 0:
  10.5 62.5 all-gather.5
  74.7 166.7 all-gather.3
  243.9 116.2 all-gather.7
  459.2 168.0 reduce-scatter.1
